TPU v7x, 32 devices: a whole 2x2x4 slice. The times are simulated.
32 devices in a mesh: bond: 8 (over z, x), mpo: 4 (over y, core).
Axes of the slice: x: 2, y: 2, z: 4, core: 2. Of those that a mesh axis runs over, the one named last changes fastest.
Arguments:
- wave_blocks: bfloat16 [8, 16, 256, 256], P('bond'), may hold values from -6 to 6
- left_environment: bfloat16 [8, 8, 256, 256], P('mpo', 'bond'), may hold values from -0.375 to 0.375
- right_environment: bfloat16 [8, 8, 256, 256], P('mpo', 'bond'), may hold values from -0.375 to 0.375
- site_operators: bfloat16 [8, 16, 16], P('mpo'), may hold values from -1.1953125 to 1.1953125
- right_sector: int32 [8, 16, 1], P('bond'), may hold values from 0 to 7; in each aligned block of 16 rows (0 to 15, 16 to 31, ..., all dimensions but the last counted through in order) at most 2 rows name the same one
- left_sizes: int32 [8], replicated, may hold values from 128 to 256
- right_sizes: int32 [8], replicated, may hold values from 128 to 256
- sector_place: int32 [8], replicated, may hold values from 0 to 7, each once
Outputs:
- applied: bfloat16 [8, 16, 256, 256], P('bond', 'mpo')
Inputs may be any that keep to these rules, and one draw needn't show every extreme that they name: `right_sector`: among the 16 blocks of one bond index no right sector is named more than 2 times, a bound that some block reaches. `sector_place`: every position is taken by exactly one right sector.
All inputs are finite; a program needn't handle non-finite values.
Results may differ from a plain program's by a relative error of at most 0.0057.
Values may be sent and summed in bfloat16 or wider, within the bound.
A program may use at most 64 MiB of HBM per device.

v0:
```python
import jax
import jax.numpy as jnp
from jax import lax
from jax.sharding import PartitionSpec as P


def lookup(entries, indices):
    count = entries.shape[0]
    matches = indices[..., None] == jnp.arange(count, dtype=jnp.int32)
    return jnp.sum(jnp.where(matches, entries, 0), axis=-1)


def shards(
    wave_blocks,
    left_environment,
    right_environment,
    site_operators,
    right_sector,
    left_sizes,
    right_sizes,
    sector_place,
):
    sectors = wave_blocks.shape[0]
    states = wave_blocks.shape[1]
    block_rows = wave_blocks.shape[2]
    channels = left_environment.shape[0]
    first_sector = lax.axis_index("bond") * sectors
    sector_ids = right_sector[:, :, 0]
    offsets = jnp.arange(block_rows, dtype=jnp.int32)
    left_live = lax.dynamic_slice_in_dim(left_sizes, first_sector, sectors)
    row_mask = offsets[None, :] < left_live[:, None]
    column_mask = offsets[None, None, :] < lookup(right_sizes, sector_ids)[:, :, None]
    live_mask = row_mask[:, None, :, None] & column_mask[:, :, None, :]
    masked = jnp.where(live_mask, wave_blocks, jnp.zeros((), jnp.bfloat16))
    block_count = sectors * states
    flat_blocks = masked.reshape(block_count, block_rows, block_rows)
    place_flat = lookup(sector_place, sector_ids).reshape(block_count)
    gathered = lax.all_gather(right_environment, "bond", axis=1, tiled=True)
    chosen = jnp.take(gathered, place_flat, axis=1)
    right_part = jnp.einsum(
        "bac,hbxc->bhax", flat_blocks, chosen, preferred_element_type=jnp.float32
    ).astype(jnp.bfloat16)
    right_part = right_part.reshape(sectors, states, channels, block_rows, block_rows)
    same_sector = sector_ids[:, :, None] == sector_ids[:, None, :]
    mixing = jnp.where(same_sector[:, None], site_operators[None], jnp.zeros((), jnp.bfloat16))
    mixed = jnp.einsum(
        "nhst,nthac->nshac", mixing, right_part, preferred_element_type=jnp.float32
    ).astype(jnp.bfloat16)
    partial_value = jnp.einsum(
        "hnab,nshbc->nsac", left_environment, mixed, preferred_element_type=jnp.float32
    )
    per_device = states // lax.axis_size("mpo")
    first_state = lax.axis_index("mpo") * per_device
    summed = lax.psum(partial_value, "mpo")
    summed = lax.dynamic_slice_in_dim(summed, first_state, per_device, 1)
    kept_mask = lax.dynamic_slice_in_dim(live_mask, first_state, per_device, 1)
    return jnp.where(kept_mask, summed, jnp.zeros((), jnp.float32)).astype(jnp.bfloat16)


def solution(mesh):
    placed = (
        P("bond", None, None, None),
        P("mpo", "bond", None, None),
        P("mpo", "bond", None, None),
        P("mpo", None, None),
        P("bond", None, None),
        P(),
        P(),
        P(),
    )
    return jax.shard_map(
        shards, mesh=mesh, in_specs=placed, out_specs=P("bond", "mpo", None, None), check_vma=False
    )
```

profile of v0, /device:TPU:0, one launch (start us, length us, event | category | flops | bytes accessed | tf_op | source)
XLA Modules:
  0.0 172.7 jit_solution(5104987714782508854)
XLA Ops:
  6.5 0.0 copy-start
  6.5 0.0 copy-start.5
  6.5 0.0 copy-start.2
  6.5 0.0 copy-start.3
  6.5 0.0 copy-start.4
  6.5 0.0 all-gather.2.cloned.1.call-start
  6.6 0.7 all-gather.2.cloned.1.call-update
  7.3 2.9 %copy.12 = bf16[1,16,256,256]{2,3,1,0:T(8,128)(2,1)S(1)} copy(bf16[1,16,256,256]{3,2,1,0:T(8,128)(2,1)} %param.8) | data formatting | bytes 4194304 | tf_op args[0]
  10.2 0.0 copy-done.5
  10.2 0.6 dynamic_slice.9
  10.8 0.6 iota_compare_fusion.2
  11.4 0.0 copy-done.2
  11.4 0.0 copy-done.3
  11.4 0.0 copy-done.4
  11.4 0.1 select_reduce_fusion.1
  11.6 0.1 broadcast_compare_fusion
  11.6 0.1 iota_compare_fusion
  11.7 2.0 %broadcast_and_fusion = pred[1,16,256,256]{2,3,1,0:T(8,128)(4,1)} fusion(pred[16,256]{1,0:T(8,128)(4,1)S(1)} %iota_compare_fusion, pred[256]{0:T(512)(128)(4,1)S(1)} %iota_compare_fusion.2), kind=kLoop, calls=%fused_computation.15 | loop fusion | flops 1048576 | bytes 1052928 | tf_op jit(solution)/shard_map/and | solution.py:33
  13.7 47.6 %all-gather.2.cloned.1.call-done = bf16[2,8,256,256]{3,2,1,0:T(8,128)(2,1)} async-done(((bf16[2,1,256,256]{3,2,1,0:T(8,128)(2,1)}), bf16[2,8,256,256]{3,2,1,0:T(8,128)(2,1)}) %all-gather.2.cloned.1.call-update) | async-done | bytes 2097168 | tf_op jit(solution)/shard_map/all_gather | solution.py:38
  61.4 4.3 %gather_fusion = bf16[16,2,256,256]{3,2,1,0:T(8,128)(2,1)} fusion(bf16[2,8,256,256]{3,2,1,0:T(8,128)(2,1)} %all-gather.2.cloned.1.call-done, s32[1024]{0:T(1024)S(1)} %pad_clamp_fusion), kind=kCustom, calls=%fused_computation | custom fusion | bytes 8388672 | tf_op jit(solution)/shard_map/jit(_take)/gather | solution.py:39
  65.7 4.7 %fusion.2 = bf16[16,2,256,256]{3,2,1,0:T(8,128)(2,1)} fusion(bf16[16,2,256,256]{3,2,1,0:T(8,128)(2,1)} %gather_fusion, pred[16]{0:T(512)(128)(4,1)S(1)} %compare_and_fusion, bf16[1,16,256,256]{2,3,1,0:T(8,128)(2,1)S(1)} %copy.12, pred[16,256]{1,0:T(8,128)(4,1)S(1)} %iota_compare_fusion, pred[256]{0:T(512)(128)(4,1)S(1)} %iota_compare_fusion.2), kind=kOutput, calls=%fused_computation.3 | convolution fusion | flops 1077936128 | bytes 10490128 | tf_op jit(solution)/shard_map/bac,hbxc->bhax/dot_general | solution.py:40
  70.4 0.0 copy-start.1
  70.4 7.9 %copy.16 = bf16[16,2,256,256]{2,0,3,1:T(8,128)(2,1)} copy(bf16[16,2,256,256]{3,2,1,0:T(8,128)(2,1)} %fusion.2) | data formatting | bytes 8388608 | tf_op jit(solution)/shard_map/bac,hbxc->bhax/dot_general | solution.py:40
  78.3 0.0 copy-done.1
  78.3 3.4 %convert_bitcast_fusion = bf16[16,2,256,256]{3,0,2,1:T(8,128)(2,1)S(1)} fusion(bf16[16,2,256,256]{2,0,3,1:T(8,128)(2,1)} %copy.16, bf16[2,16,16]{2,1,0:T(8,128)(2,1)S(1)} %copy-done.1, pred[16,16]{1,0:T(8,128)(4,1)S(1)} %broadcast_compare_fusion), kind=kOutput, calls=%fused_computation.8 | convolution fusion | flops 69206528 | bytes 8389888 | tf_op jit(solution)/shard_map/nhst,nthac->nshac/dot_general | solution.py:46
  81.7 0.0 copy-done
  81.7 6.1 %fusion.11 = f32[1,16,256,256]{2,3,1,0:T(8,128)} fusion(bf16[16,2,256,256]{3,0,2,1:T(8,128)(2,1)S(1)} %convert_bitcast_fusion, bf16[2,1,256,256]{3,2,1,0:T(8,128)(2,1)S(1)} %copy-done), kind=kOutput, calls=%fused_computation.11 | convolution fusion | flops 1073741824 | bytes 8650752 | tf_op jit(solution)/shard_map/hnab,nshbc->nsac/dot_general | solution.py:49
  87.8 75.9 %all-reduce.1 = bf16[1,16,256,256]{2,3,1,0:T(8,128)(2,1)S(1)} all-reduce(f32[1,16,256,256]{2,3,1,0:T(8,128)} %fusion.11), channel_id=1, replica_groups=mesh['bond'=8,'mpo'=4] {'mpo'}, use_global_device_ids=true, to_apply=%region_2.3 | all-reduce | flops 1048576 | bytes 6291456 | tf_op jit(solution)/shard_map/psum | solution.py:54
  163.7 1.1 select_convert_fusion
  164.8 1.0 copy.14
  (3 shorter events, 0.0 us)
Async XLA Ops:
  6.5 75.1 %copy-start = (bf16[2,1,256,256]{3,2,1,0:T(8,128)(2,1)S(1)}, bf16[2,1,256,256]{3,2,1,0:T(8,128)(2,1)}, u32[]{:S(2)}) copy-start(bf16[2,1,256,256]{3,2,1,0:T(8,128)(2,1)} %param.9) | copy-start | bytes 786436
  6.5 3.6 %copy-start.5 = (s32[8]{0:T(128)S(1)}, s32[8]{0:T(128)}, u32[]{:S(2)}) copy-start(s32[8]{0:T(128)} %param.13) | copy-start | bytes 100
  6.5 4.9 %copy-start.2 = (s32[1,16,1]{1,2,0:T(1,128)S(1)}, s32[1,16,1]{1,2,0:T(1,128)}, u32[]{:S(2)}) copy-start(s32[1,16,1]{1,2,0:T(1,128)} %param.12) | copy-start | bytes 196
  6.5 4.9 %copy-start.3 = (s32[8]{0:T(128)S(1)}, s32[8]{0:T(128)}, u32[]{:S(2)}) copy-start(s32[8]{0:T(128)} %param.14) | copy-start | bytes 100
  6.5 4.9 %copy-start.4 = (s32[8]{0:T(128)S(1)}, s32[8]{0:T(128)}, u32[]{:S(2)}) copy-start(s32[8]{0:T(128)} %param.15) | copy-start | bytes 100
  6.5 54.8 %all-gather.2.cloned.1.call-start = ((), (), s32[]{:S(2)}) async-start(), calls=%async_computation | async-start | bytes 2359296 | tf_op jit(solution)/shard_map/all_gather | solution.py:38
  70.4 7.9 %copy-start.1 = (bf16[2,16,16]{2,1,0:T(8,128)(2,1)S(1)}, bf16[2,16,16]{2,1,0:T(8,128)(2,1)}, u32[]{:S(2)}) copy-start(bf16[2,16,16]{2,1,0:T(8,128)(2,1)} %param.11) | copy-start | bytes 3076
Sparse Core Ops, SparseCore 0:
  9.5 51.7 all-gather.1
where the time goes:
time: 173 us
  blocking collectives  75.9 us (44%)
  waiting for transfers between devices  48.3 us (28%)
  local copies, waits for them, and re-layouts  16.7 us (10%)
  matrix products  14.2 us (8%)
  between operations  13.5 us (8%)
  other arithmetic  4.04 us (2%)
    psum x1, blocking collectives, shards(): summed = lax.psum(partial_value, 'mpo')  75.9 us
    all_gather x1, waiting for transfers between devices, shards(): gathered = lax.all_gather(right_environment, 'bond', axis=1, tiled=True)  47.6 us
    dot_general x1, local copies, waits for them, and re-layouts, shards(): jnp.einsum('bac,hbxc->bhax', flat_blocks, chosen, preferred_element_type=...  7.89 us
    dot_general x1, matrix products, shards(): jnp.einsum('hnab,nshbc->nsac', left_environment, mixed, preferred_element...  6.13 us
    dot_general x1, matrix products, shards(): jnp.einsum('bac,hbxc->bhax', flat_blocks, chosen, preferred_element_type=...  4.66 us
    gather x1, local copies, waits for them, and re-layouts, shards(): chosen = jnp.take(gathered, place_flat, axis=1)  4.34 us
  transfers between devices with their start and end apart: 1, of which 1 were waited for; matrix products, arithmetic and copies ran while one was open for 4% of the time, Pallas kernels for 0%

commit v1 on v0

v1 whole, which is shorter than its diff:
```python
import functools

import jax
import jax.numpy as jnp
from jax import lax
from jax.experimental import pallas as pl
from jax.experimental.pallas import tpu as pltpu
from jax.sharding import PartitionSpec as P

MESH = pl.DeviceIdType.MESH


def plane_of(count):
    nx = 1
    while (2 * nx) * (2 * nx) * 2 <= count and count % (2 * nx) == 0:
        nx *= 2
    return count // nx, nx


def kernel(
    n, m,
    sector, place, left_sizes, right_sizes, ops,
    wave_hbm, left_hbm, right_hbm,
    out_ref,
    right_all, wave, left, mixed, out_core, in_core, out_chip, in_chip, own,
    local_sem, gather_send, gather_recv, core_send, core_recv, chip_send, chip_recv,
):
    nz, nx = plane_of(n)
    cores = 2 if m % 2 == 0 else 1
    ny = m // cores
    states, rows, _ = wave.shape
    channels = left.shape[0]
    per = out_ref.shape[0]
    count = ny * per
    b = lax.axis_index("bond")
    p = lax.axis_index("mpo")
    z, x = b // nx, b % nx
    y, c = p // cores, p % cores
    sibling = y * cores + (1 - c)

    wave_copy = pltpu.make_async_copy(wave_hbm, wave, local_sem.at[0])
    left_copy = pltpu.make_async_copy(left_hbm, left, local_sem.at[1])
    own_copy = pltpu.make_async_copy(right_hbm, right_all.at[b], local_sem.at[2])
    wave_copy.start()
    left_copy.start()
    own_copy.start()

    steps = ((nx, z + 1 < nz), (-nx, z > 0), (1, x + 1 < nx), (-1, x > 0))
    barrier = pltpu.get_barrier_semaphore()
    greeted = ny
    for step, there in steps:
        greeted = greeted + there.astype(jnp.int32)

        @pl.when(there)
        def _():
            pl.semaphore_signal(barrier, inc=1, device_id=(b + step, p), device_id_type=MESH)

    pl.semaphore_signal(barrier, inc=1, device_id=(b, sibling), device_id_type=MESH)
    for dy in range(1, ny):
        other = lax.rem(y + dy, ny) * cores + c
        pl.semaphore_signal(barrier, inc=1, device_id=(b, other), device_id_type=MESH)
    pl.semaphore_wait(barrier, greeted)

    def hop(pos, h, k, src):
        return pltpu.make_async_remote_copy(
            src_ref=src,
            dst_ref=right_all.at[pos, h],
            send_sem=gather_send.at[pos, h, k],
            recv_sem=gather_recv.at[pos, h],
            device_id=(b + steps[k][0], p),
            device_id_type=MESH,
        )

    def sends(zs, xs):
        column = xs == x
        return (
            column & (zs <= z) & (z + 1 < nz),
            column & (zs >= z) & (z > 0),
            (xs <= x) & (x + 1 < nx),
            (xs >= x) & (x > 0),
        )

    def forward(zs, xs, h):
        pos = zs * nx + xs
        for k, wanted in enumerate(sends(zs, xs)):
            @pl.when(wanted)
            def _():
                hop(pos, h, k, right_all.at[pos, h]).start()

    def arrived(pos, h):
        hop(pos, h, 0, right_all.at[pos, h]).wait_recv()

    for h in range(channels):
        for k in (0, 1, 2, 3):
            @pl.when(steps[k][1])
            def _():
                hop(b, h, k, right_hbm.at[h]).start()

    wave_copy.wait()
    left_copy.wait()
    own_copy.wait()

    row_index = lax.broadcasted_iota(jnp.int32, (rows, rows), 0)
    column_index = lax.broadcasted_iota(jnp.int32, (rows, rows), 1)
    live_rows = row_index < left_sizes[b]

    def work(pos):
        def look(s, carry):
            first, last, hits = carry
            hit = place[sector[s]] == pos
            first = jnp.where(hit & (hits == 0), s, first)
            last = jnp.where(hit, s, last)
            return first, last, hits + hit.astype(jnp.int32)

        zero = jnp.int32(0)
        s1, s2, hits = lax.fori_loop(0, states, look, (zero, zero, zero), unroll=True)
        live = live_rows & (column_index < right_sizes[sector[s1]])

        def masked(s):
            return jnp.where(live, wave[s].astype(jnp.float32), 0.0).astype(jnp.bfloat16)

        w1, w2 = masked(s1), masked(s2)
        two = hits == 2
        for h in range(channels):
            factor = right_all[pos, h]

            def right_part(w):
                part = lax.dot_general(
                    w, factor, (((1,), (1,)), ((), ())), preferred_element_type=jnp.float32
                )
                return part.astype(jnp.bfloat16).astype(jnp.float32)

            def op(s, t):
                return ops[(h * states + s) * states + t]

            p1, p2 = right_part(w1), right_part(w2)
            o12, o21 = jnp.where(two, op(s1, s2), 0.0), jnp.where(two, op(s2, s1), 0.0)
            mixed[2 * pos, h] = (op(s1, s1) * p1 + o12 * p2).astype(jnp.bfloat16)
            mixed[2 * pos + 1, h] = (o21 * p1 + op(s2, s2) * p2).astype(jnp.bfloat16)

    def gather_round(d, _):
        @pl.when((d > 0) & (d < nz))
        def _():
            for h in range(channels):
                for sign in (1, -1):
                    zs = z + sign * d

                    @pl.when((zs >= 0) & (zs < nz))
                    def _():
                        arrived(zs * nx + x, h)
                        forward(zs, x, h)

        def one(i, _):
            sign = 1 - 2 * (i % 2)
            e = i // 2
            offset = (e + 1) // 2 * (1 - 2 * (e % 2))
            zs = z + sign * (d - 1)
            xs = x + offset

            @pl.when((zs >= 0) & (zs < nz) & (xs >= 0) & (xs < nx) & ((d > 1) | (sign > 0)))
            def _():
                pos = zs * nx + xs

                @pl.when(xs != x)
                def _():
                    for h in range(channels):
                        arrived(pos, h)
                        forward(zs, xs, h)

                work(pos)

            return 0

        @pl.when(d > 0)
        def _():
            lax.fori_loop(0, 2 * (2 * nx - 1), one, 0)

        return 0

    lax.fori_loop(1, nz + 1, gather_round, 0)

    def product(s):
        def look(t, rank):
            return rank + ((t < s) & (sector[t] == sector[s])).astype(jnp.int32)

        rank = lax.fori_loop(0, states, look, jnp.int32(0), unroll=True)
        slot = 2 * place[sector[s]] + rank
        total = jnp.dot(left[0], mixed[slot, 0], preferred_element_type=jnp.float32)
        for h in range(1, channels):
            total += jnp.dot(left[h], mixed[slot, h], preferred_element_type=jnp.float32)
        return total

    def owner_chip(i):
        return lax.rem(y + 1 + i // per, ny)

    def to_core(i):
        return pltpu.make_async_remote_copy(
            src_ref=out_core.at[i], dst_ref=in_core.at[i],
            send_sem=core_send.at[i], recv_sem=core_recv.at[i],
            device_id=(b, sibling), device_id_type=MESH,
        )

    def to_chip(i):
        return pltpu.make_async_remote_copy(
            src_ref=out_chip.at[i], dst_ref=in_chip.at[i],
            send_sem=chip_send.at[i], recv_sem=chip_recv.at[i],
            device_id=(b, owner_chip(i) * cores + c), device_id_type=MESH,
        )

    remote = (ny - 1) * per
    lag = min(3, count)

    def reduce_step(i, _):
        @pl.when(i < count)
        def _():
            s = (owner_chip(i) * cores + (1 - c)) * per + i % per
            out_core[i] = product(s).astype(jnp.bfloat16)
            to_core(i).start()

        @pl.when(i >= lag)
        def _():
            j = i - lag
            s = (owner_chip(j) * cores + c) * per + j % per
            total = product(s)
            to_core(j).wait_recv()
            total = total + in_core[j].astype(jnp.float32)

            @pl.when(j < remote)
            def _():
                out_chip[j] = total.astype(jnp.bfloat16)
                to_chip(j).start()

            @pl.when(j >= remote)
            def _():
                own[j - remote] = total

        return 0

    lax.fori_loop(0, count + lag, reduce_step, 0)

    for q in range(per):
        total = own[q]
        for dy in range(ny - 1):
            to_chip(dy * per + q).wait_recv()
            total = total + in_chip[dy * per + q].astype(jnp.float32)
        live = live_rows & (column_index < right_sizes[sector[p * per + q]])
        out_ref[q] = jnp.where(live, total, 0.0).astype(jnp.bfloat16)

    def finish(pos, _):
        for k, wanted in enumerate(sends(pos // nx, pos % nx)):
            @pl.when(wanted)
            def _():
                for h in range(channels):
                    hop(pos, h, k, right_all.at[pos, h]).wait_send()
        return 0

    lax.fori_loop(0, n, finish, 0)

    def finish_core(i, _):
        to_core(i).wait_send()
        return 0

    lax.fori_loop(0, count, finish_core, 0)

    def finish_chip(i, _):
        to_chip(i).wait_send()
        return 0

    lax.fori_loop(0, remote, finish_chip, 0)


def shards(n, m, wave_blocks, left_environment, right_environment, site_operators,
           right_sector, left_sizes, right_sizes, sector_place):
    states, rows = wave_blocks.shape[1:3]
    channels = left_environment.shape[0]
    per = states // m
    cores = 2 if m % 2 == 0 else 1
    ny = m // cores
    count = ny * per
    remote = max(1, (ny - 1) * per)
    block = (rows, rows)
    bf16, f32 = jnp.bfloat16, jnp.float32
    smem = pl.BlockSpec(memory_space=pltpu.SMEM)
    hbm = pl.BlockSpec(memory_space=pl.ANY)
    out = pl.pallas_call(
        functools.partial(kernel, n, m),
        out_shape=jax.ShapeDtypeStruct((per,) + block, bf16),
        in_specs=[smem] * 5 + [hbm] * 3,
        out_specs=pl.BlockSpec(memory_space=pltpu.VMEM),
        scratch_shapes=[
            pltpu.VMEM((n, channels) + block, bf16),
            pltpu.VMEM((states,) + block, bf16),
            pltpu.VMEM((channels,) + block, bf16),
            pltpu.VMEM((2 * n, channels) + block, bf16),
            pltpu.VMEM((count,) + block, bf16),
            pltpu.VMEM((count,) + block, bf16),
            pltpu.VMEM((remote,) + block, bf16),
            pltpu.VMEM((remote,) + block, bf16),
            pltpu.VMEM((per,) + block, f32),
            pltpu.SemaphoreType.DMA((3,)),
            pltpu.SemaphoreType.DMA((n, channels, 4)),
            pltpu.SemaphoreType.DMA((n, channels)),
            pltpu.SemaphoreType.DMA((count,)),
            pltpu.SemaphoreType.DMA((count,)),
            pltpu.SemaphoreType.DMA((remote,)),
            pltpu.SemaphoreType.DMA((remote,)),
        ],
        compiler_params=pltpu.CompilerParams(
            collective_id=0, has_side_effects=True, vmem_limit_bytes=60 * 1024 * 1024
        ),
    )(
        right_sector.reshape(states), sector_place, left_sizes, right_sizes,
        site_operators.astype(f32).reshape(channels * states * states),
        wave_blocks.reshape((states,) + block),
        left_environment.reshape((channels,) + block),
        right_environment.reshape((channels,) + block),
    )
    return out.reshape((1, per) + block)


def solution(mesh):
    placed = (
        P("bond", None, None, None),
        P("mpo", "bond", None, None),
        P("mpo", "bond", None, None),
        P("mpo", None, None),
        P("bond", None, None),
        P(),
        P(),
        P(),
    )
    body = functools.partial(shards, mesh.shape["bond"], mesh.shape["mpo"])
    return jax.shard_map(
        body, mesh=mesh, in_specs=placed, out_specs=P("bond", "mpo", None, None), check_vma=False
    )
```

time: 173 us -> 49.6 us (0.29)
  blocking collectives: 75.9 us -> 0 us
  waiting for transfers between devices: 48.3 us -> 0 us
  Pallas kernels: 0 us -> 46.2 us
  matrix products: 14.2 us -> 0 us
  between operations: 13.5 us -> 0.01 us
  local copies, waits for them, and re-layouts: 16.7 us -> 3.23 us
  other arithmetic: 4.04 us -> 0 us
    psum x1 -> x0, blocking collectives: 75.9 us -> none  [shards(): summed = lax.psum(partial_value, 'mpo')]
    all_gather x1 -> x0, waiting for transfers between devices: 47.6 us -> none  [shards(): gathered = lax.all_gather(right_environment, 'bond', axis=1, tiled=True)]
    pallas_call x0 -> x1, Pallas kernels: none -> 46.2 us  [shards(): pl.pallas_call(functools.partial(kernel, n, m), out_shape=jax.ShapeDtypeS...]
    dot_general x3 -> x0, matrix products: 14.2 us -> none  [the longest x1 6.13 us: shards(): jnp.einsum('hnab,nshbc->nsac', left_environment, mixed, preferred_element...]
    dot_general x1 -> x0, local copies, waits for them, and re-layouts: 7.89 us -> none  [shards(): jnp.einsum('bac,hbxc->bhax', flat_blocks, chosen, preferred_element_type=...]
    gather x1 -> x0, local copies, waits for them, and re-layouts: 4.34 us -> none  [shards(): chosen = jnp.take(gathered, place_flat, axis=1)]
    and x2 -> x0, other arithmetic: 2.02 us -> none  [the longest x1 2.02 us: shards(): live_mask = row_mask[:, None, :, None] & column_mask[:, :, None, :]]
  transfers between devices with their start and end apart: 1 -> 0, of which waited for: 1 -> 0; matrix products, arithmetic and copies ran while one was open for 4% -> 0% of each run, Pallas kernels for 0% -> 0%
where the time goes in v1:
time: 49.6 us; the launch traced here: 49.4 us
  Pallas kernels  46.2 us (93%)
  local copies, waits for them, and re-layouts  3.23 us (7%)
    pallas_call x1, Pallas kernels, shards(): pl.pallas_call(functools.partial(kernel, n, m), out_shape=jax.ShapeDtypeS...  46.2 us
    unnamed x1, local copies, waits for them, and re-layouts  1.87 us
    reshape x1, local copies, waits for them, and re-layouts, shards(): site_operators.astype(f32).reshape(channels * states * states)  1.36 us

profile of v1, /device:TPU:0, one launch (start us, length us, event | category | flops | bytes accessed | tf_op | source)
XLA Modules:
  0.0 49.4 jit_solution(13732990968151883285)
XLA Ops:
  0.0 1.4 %reshape.28.ops = f32[512]{0:T(512)} reshape(bf16[2,16,16]{2,1,0:T(8,128)(2,1)} %param.11) | data formatting | bytes 3072 | tf_op jit(solution)/shard_map/reshape | solution.py:313
  1.4 46.2 %shard_map.82 = bf16[4,256,256]{2,1,0:T(8,128)(2,1)} custom-call(s32[16]{0:T(128)} %bitcast.9, s32[8]{0:T(128)} %place.1, s32[8]{0:T(128)} %left_sizes.1, s32[8]{0:T(128)} %right_sizes.1, f32[512]{0:T(512)} %reshape.28.ops, bf16[16,256,256]{2,1,0:T(8,128)(2,1)} %bitcast.5, bf16[2,256,256]{2,1,0:T(8,128)(2,1)} %bitcast.7, bf16[2,256,256]{2,1,0:T(8,128)(2,1)} %bitcast.8), custom_call_target="tpu_custom_call" | custom-call | tf_op jit(solution)/shard_map/pallas_call | solution.py:285
  47.5 1.9 %copy.10 = bf16[1,4,256,256]{3,2,1,0:T(8,128)(2,1)} copy(bf16[1,4,256,256]{3,2,1,0:T(8,128)(2,1)} %bitcast.6) | data formatting | bytes 1048576

commit v2 on v1

--- a/solution.py
+++ b/solution.py
@@ -22,8 +22,7 @@
     sector, place, left_sizes, right_sizes, ops,
     wave_hbm, left_hbm, right_hbm,
     out_ref,
-    right_all, wave, left, mixed, out_core, in_core, out_chip, in_chip, own,
-    local_sem, gather_send, gather_recv, core_send, core_recv, chip_send, chip_recv,
+    right_all, wave, left, local_sem, gather_send, gather_recv, *rest,
 ):
     nz, nx = plane_of(n)
     cores = 2 if m % 2 == 0 else 1
@@ -32,6 +31,13 @@
     channels = left.shape[0]
     per = out_ref.shape[0]
     count = ny * per
+    pair = ny == 2 and cores == 2
+    if pair:
+        (part, part_out, part_in, sums,
+         part_send, part_recv, sum_send, sum_recv) = rest
+    else:
+        (mixed, out_core, in_core, out_chip, in_chip, own,
+         core_send, core_recv, chip_send, chip_recv) = rest
     b = lax.axis_index("bond")
     p = lax.axis_index("mpo")
     z, x = b // nx, b % nx
@@ -103,6 +109,41 @@
     row_index = lax.broadcasted_iota(jnp.int32, (rows, rows), 0)
     column_index = lax.broadcasted_iota(jnp.int32, (rows, rows), 1)
     live_rows = row_index < left_sizes[b]
+    op_row = lax.broadcasted_iota(jnp.int32, (states, states), 0)
+    op_column = lax.broadcasted_iota(jnp.int32, (states, states), 1)
+
+    def to_sibling(pos):
+        return pltpu.make_async_remote_copy(
+            src_ref=part_out.at[pos], dst_ref=part_in.at[pos],
+            send_sem=part_send.at[pos], recv_sem=part_recv.at[pos],
+            device_id=(b, sibling), device_id_type=MESH,
+        )
+
+    def share(kind, pos):
+        source, target = (0, 0, 1)[kind], (0, 1, 1)[kind]
+        device = (1 - y) * cores + c if kind == 1 else sibling
+        return pltpu.make_async_remote_copy(
+            src_ref=sums.at[source, pos, c], dst_ref=sums.at[target, pos, c],
+            send_sem=sum_send.at[kind, pos], recv_sem=sum_recv.at[target, pos, c],
+            device_id=(b, device), device_id_type=MESH,
+        )
+
+    def sum_arrived(target, pos, rank):
+        pltpu.make_async_remote_copy(
+            src_ref=sums.at[target, pos, rank], dst_ref=sums.at[target, pos, rank],
+            send_sem=sum_send.at[0, pos], recv_sem=sum_recv.at[target, pos, rank],
+            device_id=(b, sibling), device_id_type=MESH,
+        ).wait_recv()
+
+    def add_up(pos):
+        to_sibling(pos).wait_recv()
+        sums[0, pos, c] = (part[pos] + part_in[pos].astype(jnp.float32)).astype(jnp.bfloat16)
+        share(1, pos).start()
+        share(0, pos).start()
+
+    def pass_on(pos):
+        sum_arrived(1, pos, c)
+        share(2, pos).start()
 
     def work(pos):
         def look(s, carry):
@@ -114,6 +155,8 @@
 
         zero = jnp.int32(0)
         s1, s2, hits = lax.fori_loop(0, states, look, (zero, zero, zero), unroll=True)
+        if pair:
+            s1, s2 = jnp.where(c == 0, s1, s2), jnp.where(c == 0, s2, s1)
         live = live_rows & (column_index < right_sizes[sector[s1]])
 
         def masked(s):
@@ -130,13 +173,27 @@
                 )
                 return part.astype(jnp.bfloat16).astype(jnp.float32)
 
-            def op(s, t):
-                return ops[(h * states + s) * states + t]
+            table = ops[h].astype(jnp.float32)
+
+            def op(s, t, keep=True):
+                picked = (op_row == s) & (op_column == t) & keep
+                return jnp.sum(jnp.where(picked, table, 0.0), keepdims=True)
 
             p1, p2 = right_part(w1), right_part(w2)
-            o12, o21 = jnp.where(two, op(s1, s2), 0.0), jnp.where(two, op(s2, s1), 0.0)
-            mixed[2 * pos, h] = (op(s1, s1) * p1 + o12 * p2).astype(jnp.bfloat16)
-            mixed[2 * pos + 1, h] = (o21 * p1 + op(s2, s2) * p2).astype(jnp.bfloat16)
+            m1 = (op(s1, s1) * p1 + op(s1, s2, two) * p2).astype(jnp.bfloat16)
+            m2 = (op(s2, s1, two) * p1 + op(s2, s2) * p2).astype(jnp.bfloat16)
+            if pair:
+                left_m = left[h]
+                q1 = jnp.dot(left_m, m1, preferred_element_type=jnp.float32)
+                q2 = jnp.dot(left_m, m2, preferred_element_type=jnp.float32)
+                total1, total2 = (q1, q2) if h == 0 else (total1 + q1, total2 + q2)
+            else:
+                mixed[2 * pos, h] = m1
+                mixed[2 * pos + 1, h] = m2
+        if pair:
+            part_out[pos] = total2.astype(jnp.bfloat16)
+            to_sibling(pos).start()
+            part[pos] = total1
 
     def gather_round(d, _):
         @pl.when((d > 0) & (d < nz))
@@ -150,41 +207,83 @@
                         arrived(zs * nx + x, h)
                         forward(zs, x, h)
 
-        def one(i, _):
-            sign = 1 - 2 * (i % 2)
-            e = i // 2
-            offset = (e + 1) // 2 * (1 - 2 * (e % 2))
-            zs = z + sign * (d - 1)
-            xs = x + offset
-
-            @pl.when((zs >= 0) & (zs < nz) & (xs >= 0) & (xs < nx) & ((d > 1) | (sign > 0)))
-            def _():
-                pos = zs * nx + xs
-
-                @pl.when(xs != x)
+        def each(d, body):
+            def one(i, _):
+                sign = 1 - 2 * (i % 2)
+                e = i // 2
+                zs = z + sign * d
+                xs = x + (e + 1) // 2 * (1 - 2 * (e % 2))
+
+                @pl.when((zs >= 0) & (zs < nz) & (xs >= 0) & (xs < nx) & ((d > 0) | (sign > 0)))
                 def _():
-                    for h in range(channels):
-                        arrived(pos, h)
-                        forward(zs, xs, h)
-
-                work(pos)
-
-            return 0
-
-        @pl.when(d > 0)
+                    body(zs, xs)
+
+                return 0
+
+            lax.fori_loop(0, 2 * (2 * nx - 1), one, 0)
+
+        def use(zs, xs):
+            pos = zs * nx + xs
+
+            @pl.when(xs != x)
+            def _():
+                for h in range(channels):
+                    arrived(pos, h)
+                    forward(zs, xs, h)
+
+            work(pos)
+
+        @pl.when(d <= nz)
         def _():
-            lax.fori_loop(0, 2 * (2 * nx - 1), one, 0)
+            each(d - 1, use)
+            if pair:
+                each(d - 1, lambda zs, xs: add_up(zs * nx + xs))
+
+        if pair:
+            @pl.when(d > 1)
+            def _():
+                each(d - 2, lambda zs, xs: pass_on(zs * nx + xs))
 
         return 0
 
-    lax.fori_loop(1, nz + 1, gather_round, 0)
-
-    def product(s):
+    lax.fori_loop(1, nz + (2 if pair else 1), gather_round, 0)
+
+    def rank_of(s):
         def look(t, rank):
             return rank + ((t < s) & (sector[t] == sector[s])).astype(jnp.int32)
 
-        rank = lax.fori_loop(0, states, look, jnp.int32(0), unroll=True)
-        slot = 2 * place[sector[s]] + rank
+        return jnp.minimum(lax.fori_loop(0, states, look, jnp.int32(0), unroll=True), 1)
+
+    def finish(pos, _):
+        for k, wanted in enumerate(sends(pos // nx, pos % nx)):
+            @pl.when(wanted)
+            def _():
+                for h in range(channels):
+                    hop(pos, h, k, right_all.at[pos, h]).wait_send()
+        if pair:
+            to_sibling(pos).wait_send()
+            for kind in range(3):
+                share(kind, pos).wait_send()
+        return 0
+
+    if pair:
+        def all_here(pos, _):
+            sum_arrived(0, pos, 1 - c)
+            sum_arrived(1, pos, 1 - c)
+            return 0
+
+        lax.fori_loop(0, n, all_here, 0)
+        for q in range(per):
+            s = p * per + q
+            at, rank = place[sector[s]], rank_of(s)
+            total = sums[0, at, rank].astype(jnp.float32) + sums[1, at, rank].astype(jnp.float32)
+            live = live_rows & (column_index < right_sizes[sector[s]])
+            out_ref[q] = jnp.where(live, total, 0.0).astype(jnp.bfloat16)
+        lax.fori_loop(0, n, finish, 0)
+        return
+
+    def product(s):
+        slot = 2 * place[sector[s]] + rank_of(s)
         total = jnp.dot(left[0], mixed[slot, 0], preferred_element_type=jnp.float32)
         for h in range(1, channels):
             total += jnp.dot(left[h], mixed[slot, h], preferred_element_type=jnp.float32)
@@ -245,14 +344,6 @@
             total = total + in_chip[dy * per + q].astype(jnp.float32)
         live = live_rows & (column_index < right_sizes[sector[p * per + q]])
         out_ref[q] = jnp.where(live, total, 0.0).astype(jnp.bfloat16)
-
-    def finish(pos, _):
-        for k, wanted in enumerate(sends(pos // nx, pos % nx)):
-            @pl.when(wanted)
-            def _():
-                for h in range(channels):
-                    hop(pos, h, k, right_all.at[pos, h]).wait_send()
-        return 0
 
     lax.fori_loop(0, n, finish, 0)
 
@@ -282,35 +373,45 @@
     bf16, f32 = jnp.bfloat16, jnp.float32
     smem = pl.BlockSpec(memory_space=pltpu.SMEM)
     hbm = pl.BlockSpec(memory_space=pl.ANY)
-    out = pl.pallas_call(
-        functools.partial(kernel, n, m),
-        out_shape=jax.ShapeDtypeStruct((per,) + block, bf16),
-        in_specs=[smem] * 5 + [hbm] * 3,
-        out_specs=pl.BlockSpec(memory_space=pltpu.VMEM),
-        scratch_shapes=[
-            pltpu.VMEM((n, channels) + block, bf16),
-            pltpu.VMEM((states,) + block, bf16),
-            pltpu.VMEM((channels,) + block, bf16),
+    dma = pltpu.SemaphoreType.DMA
+    if ny == 2 and cores == 2:
+        rest = [
+            pltpu.VMEM((n,) + block, f32),
+            pltpu.VMEM((n,) + block, bf16),
+            pltpu.VMEM((n,) + block, bf16),
+            pltpu.VMEM((2, n, 2) + block, bf16),
+            dma((n,)), dma((n,)), dma((3, n)), dma((2, n, 2)),
+        ]
+    else:
+        rest = [
             pltpu.VMEM((2 * n, channels) + block, bf16),
             pltpu.VMEM((count,) + block, bf16),
             pltpu.VMEM((count,) + block, bf16),
             pltpu.VMEM((remote,) + block, bf16),
             pltpu.VMEM((remote,) + block, bf16),
             pltpu.VMEM((per,) + block, f32),
+            dma((count,)), dma((count,)), dma((remote,)), dma((remote,)),
+        ]
+    out = pl.pallas_call(
+        functools.partial(kernel, n, m),
+        out_shape=jax.ShapeDtypeStruct((per,) + block, bf16),
+        in_specs=[smem] * 4 + [pl.BlockSpec(memory_space=pltpu.VMEM)] + [hbm] * 3,
+        out_specs=pl.BlockSpec(memory_space=pltpu.VMEM),
+        scratch_shapes=[
+            pltpu.VMEM((n, channels) + block, bf16),
+            pltpu.VMEM((states,) + block, bf16),
+            pltpu.VMEM((channels,) + block, bf16),
             pltpu.SemaphoreType.DMA((3,)),
             pltpu.SemaphoreType.DMA((n, channels, 4)),
             pltpu.SemaphoreType.DMA((n, channels)),
-            pltpu.SemaphoreType.DMA((count,)),
-            pltpu.SemaphoreType.DMA((count,)),
-            pltpu.SemaphoreType.DMA((remote,)),
-            pltpu.SemaphoreType.DMA((remote,)),
+            *rest,
         ],
         compiler_params=pltpu.CompilerParams(
             collective_id=0, has_side_effects=True, vmem_limit_bytes=60 * 1024 * 1024
         ),
     )(
         right_sector.reshape(states), sector_place, left_sizes, right_sizes,
-        site_operators.astype(f32).reshape(channels * states * states),
+        site_operators,
         wave_blocks.reshape((states,) + block),
         left_environment.reshape((channels,) + block),
         right_environment.reshape((channels,) + block),

time: 49.6 us -> 46.5 us (0.938)
  the two profiles are of different devices: /device:TPU:0 before, /device:TPU:17 now
where the time goes in v2:
time: 46.5 us; the launch traced here: 46.3 us
  Pallas kernels  44.5 us (96%)
  local copies, waits for them, and re-layouts  1.87 us (4%)
    pallas_call x1, Pallas kernels, shards(): pl.pallas_call(functools.partial(kernel, n, m), out_shape=jax.ShapeDtypeS...  44.5 us
    unnamed x1, local copies, waits for them, and re-layouts  1.87 us

profile of v2, /device:TPU:17, one launch (start us, length us, event | category | flops | bytes accessed | tf_op | source)
XLA Modules:
  0.0 46.3 jit_solution(11648787915304215169)
XLA Ops:
  0.0 44.5 %shard_map.82 = bf16[4,256,256]{2,1,0:T(8,128)(2,1)} custom-call(s32[16]{0:T(128)} %bitcast.9, s32[8]{0:T(128)} %place.1, s32[8]{0:T(128)} %left_sizes.1, s32[8]{0:T(128)} %right_sizes.1, bf16[2,16,16]{2,1,0:T(8,128)(2,1)} %ops.1, bf16[16,256,256]{2,1,0:T(8,128)(2,1)} %bitcast.5, bf16[2,256,256]{2,1,0:T(8,128)(2,1)} %bitcast.7, bf16[2,256,256]{2,1,0:T(8,128)(2,1)} %bitcast.8), custom_call_target="tpu_custom_call" | custom-call | tf_op jit(solution)/shard_map/pallas_call | solution.py:395
  44.5 1.9 %copy.10 = bf16[1,4,256,256]{3,2,1,0:T(8,128)(2,1)} copy(bf16[1,4,256,256]{3,2,1,0:T(8,128)(2,1)} %bitcast.6) | data formatting | bytes 1048576

commit v3 on v2

--- a/solution.py
+++ b/solution.py
@@ -77,18 +77,23 @@
             device_id_type=MESH,
         )
 
-    def sends(zs, xs):
+    def sends(zs, xs, h):
         column = xs == x
+        if nx == 2 and h == channels - 1 and channels > 1:
+            detour = (zs == 0) | (zs == nz - 1)
+            along, across = column | detour, ~detour | (zs == z)
+        else:
+            along, across = column, True
         return (
-            column & (zs <= z) & (z + 1 < nz),
-            column & (zs >= z) & (z > 0),
-            (xs <= x) & (x + 1 < nx),
-            (xs >= x) & (x > 0),
+            along & (zs <= z) & (z + 1 < nz),
+            along & (zs >= z) & (z > 0),
+            across & (xs <= x) & (x + 1 < nx),
+            across & (xs >= x) & (x > 0),
         )
 
     def forward(zs, xs, h):
         pos = zs * nx + xs
-        for k, wanted in enumerate(sends(zs, xs)):
+        for k, wanted in enumerate(sends(zs, xs, h)):
             @pl.when(wanted)
             def _():
                 hop(pos, h, k, right_all.at[pos, h]).start()
@@ -195,58 +200,59 @@
             to_sibling(pos).start()
             part[pos] = total1
 
-    def gather_round(d, _):
-        @pl.when((d > 0) & (d < nz))
+    def each(g, body):
+        def one(i, _):
+            sign = 1 - 2 * (i % 2)
+            e = i // 2
+            d = g - (e > 0).astype(jnp.int32)
+            zs = z + sign * d
+            xs = x + (e + 1) // 2 * (1 - 2 * (e % 2))
+
+            @pl.when((zs >= 0) & (zs < nz) & (xs >= 0) & (xs < nx) & (d >= 0) & ((d > 0) | (sign > 0)))
+            def _():
+                body(zs, xs)
+
+            return 0
+
+        lax.fori_loop(0, 2 * (2 * nx - 1), one, 0)
+
+    def use(zs, xs):
+        pos = zs * nx + xs
+
+        @pl.when(xs != x)
+        def _():
+            for h in range(channels):
+                arrived(pos, h)
+                forward(zs, xs, h)
+
+        work(pos)
+
+    def gather_round(g, _):
+        @pl.when((g > 0) & (g < nz))
         def _():
             for h in range(channels):
                 for sign in (1, -1):
-                    zs = z + sign * d
+                    zs = z + sign * g
 
                     @pl.when((zs >= 0) & (zs < nz))
                     def _():
                         arrived(zs * nx + x, h)
                         forward(zs, x, h)
 
-        def each(d, body):
-            def one(i, _):
-                sign = 1 - 2 * (i % 2)
-                e = i // 2
-                zs = z + sign * d
-                xs = x + (e + 1) // 2 * (1 - 2 * (e % 2))
-
-                @pl.when((zs >= 0) & (zs < nz) & (xs >= 0) & (xs < nx) & ((d > 0) | (sign > 0)))
-                def _():
-                    body(zs, xs)
-
-                return 0
-
-            lax.fori_loop(0, 2 * (2 * nx - 1), one, 0)
-
-        def use(zs, xs):
-            pos = zs * nx + xs
-
-            @pl.when(xs != x)
-            def _():
-                for h in range(channels):
-                    arrived(pos, h)
-                    forward(zs, xs, h)
-
-            work(pos)
-
-        @pl.when(d <= nz)
-        def _():
-            each(d - 1, use)
+        @pl.when(g <= nz)
+        def _():
+            each(g, use)
             if pair:
-                each(d - 1, lambda zs, xs: add_up(zs * nx + xs))
+                each(g, lambda zs, xs: add_up(zs * nx + xs))
 
         if pair:
-            @pl.when(d > 1)
-            def _():
-                each(d - 2, lambda zs, xs: pass_on(zs * nx + xs))
+            @pl.when(g > 1)
+            def _():
+                each(g - 2, lambda zs, xs: pass_on(zs * nx + xs))
 
         return 0
 
-    lax.fori_loop(1, nz + (2 if pair else 1), gather_round, 0)
+    lax.fori_loop(0, nz + (3 if pair else 1), gather_round, 0)
 
     def rank_of(s):
         def look(t, rank):
@@ -255,10 +261,10 @@
         return jnp.minimum(lax.fori_loop(0, states, look, jnp.int32(0), unroll=True), 1)
 
     def finish(pos, _):
-        for k, wanted in enumerate(sends(pos // nx, pos % nx)):
-            @pl.when(wanted)
-            def _():
-                for h in range(channels):
+        for h in range(channels):
+            for k, wanted in enumerate(sends(pos // nx, pos % nx, h)):
+                @pl.when(wanted)
+                def _():
                     hop(pos, h, k, right_all.at[pos, h]).wait_send()
         if pair:
             to_sibling(pos).wait_send()

time: 46.5 us -> 42.9 us (0.923)
  the two profiles are of different devices: /device:TPU:17 before, /device:TPU:0 now
where the time goes in v3:
time: 42.9 us; the launch traced here: 42.5 us
  Pallas kernels  40.6 us (95%)
  local copies, waits for them, and re-layouts  1.87 us (4%)
    pallas_call x1, Pallas kernels, shards(): pl.pallas_call(functools.partial(kernel, n, m), out_shape=jax.ShapeDtypeS...  40.6 us
    unnamed x1, local copies, waits for them, and re-layouts  1.87 us

profile of v3, /device:TPU:0, one launch (start us, length us, event | category | flops | bytes accessed | tf_op | source)
XLA Modules:
  0.0 42.5 jit_solution(15854897769999319171)
XLA Ops:
  0.0 40.6 %shard_map.82 = bf16[4,256,256]{2,1,0:T(8,128)(2,1)} custom-call(s32[16]{0:T(128)} %bitcast.9, s32[8]{0:T(128)} %place.1, s32[8]{0:T(128)} %left_sizes.1, s32[8]{0:T(128)} %right_sizes.1, bf16[2,16,16]{2,1,0:T(8,128)(2,1)} %ops.1, bf16[16,256,256]{2,1,0:T(8,128)(2,1)} %bitcast.5, bf16[2,256,256]{2,1,0:T(8,128)(2,1)} %bitcast.7, bf16[2,256,256]{2,1,0:T(8,128)(2,1)} %bitcast.8), custom_call_target="tpu_custom_call" | custom-call | tf_op jit(solution)/shard_map/pallas_call | solution.py:401
  40.6 1.9 %copy.10 = bf16[1,4,256,256]{3,2,1,0:T(8,128)(2,1)} copy(bf16[1,4,256,256]{3,2,1,0:T(8,128)(2,1)} %bitcast.6) | data formatting | bytes 1048576

commit v4 on v3

--- a/solution.py
+++ b/solution.py
@@ -167,24 +167,21 @@
         def masked(s):
             return jnp.where(live, wave[s].astype(jnp.float32), 0.0).astype(jnp.bfloat16)
 
-        w1, w2 = masked(s1), masked(s2)
+        both = jnp.concatenate([masked(s1), masked(s2)], axis=0)
         two = hits == 2
         for h in range(channels):
             factor = right_all[pos, h]
 
-            def right_part(w):
-                part = lax.dot_general(
-                    w, factor, (((1,), (1,)), ((), ())), preferred_element_type=jnp.float32
-                )
-                return part.astype(jnp.bfloat16).astype(jnp.float32)
-
+            parts = lax.dot_general(
+                both, factor, (((1,), (1,)), ((), ())), preferred_element_type=jnp.float32
+            ).astype(jnp.bfloat16).astype(jnp.float32)
+            p1, p2 = parts[:rows], parts[rows:]
             table = ops[h].astype(jnp.float32)
 
             def op(s, t, keep=True):
                 picked = (op_row == s) & (op_column == t) & keep
                 return jnp.sum(jnp.where(picked, table, 0.0), keepdims=True)
 
-            p1, p2 = right_part(w1), right_part(w2)
             m1 = (op(s1, s1) * p1 + op(s1, s2, two) * p2).astype(jnp.bfloat16)
             m2 = (op(s2, s1, two) * p1 + op(s2, s2) * p2).astype(jnp.bfloat16)
             if pair:
@@ -200,21 +197,39 @@
             to_sibling(pos).start()
             part[pos] = total1
 
+    def at(g, i, body):
+        sign = 1 - 2 * (i % 2)
+        e = i // 2
+        d = g - (e > 0).astype(jnp.int32)
+        zs = z + sign * d
+        xs = x + (e + 1) // 2 * (1 - 2 * (e % 2))
+
+        @pl.when((zs >= 0) & (zs < nz) & (xs >= 0) & (xs < nx) & (d >= 0) & ((d > 0) | (sign > 0)))
+        def _():
+            body(zs, xs)
+
+    items = 2 * (2 * nx - 1)
+
     def each(g, body):
         def one(i, _):
-            sign = 1 - 2 * (i % 2)
-            e = i // 2
-            d = g - (e > 0).astype(jnp.int32)
-            zs = z + sign * d
-            xs = x + (e + 1) // 2 * (1 - 2 * (e % 2))
-
-            @pl.when((zs >= 0) & (zs < nz) & (xs >= 0) & (xs < nx) & (d >= 0) & ((d > 0) | (sign > 0)))
-            def _():
-                body(zs, xs)
-
+            at(g, i, body)
             return 0
 
-        lax.fori_loop(0, 2 * (2 * nx - 1), one, 0)
+        lax.fori_loop(0, items, one, 0)
+
+    def multiply(g):
+        def one(i, _):
+            @pl.when(i < items)
+            def _():
+                at(g, i, use)
+
+            @pl.when(i >= 2)
+            def _():
+                at(g, i - 2, lambda zs, xs: add_up(zs * nx + xs))
+
+            return 0
+
+        lax.fori_loop(0, items + 2, one, 0)
 
     def use(zs, xs):
         pos = zs * nx + xs
@@ -241,9 +256,10 @@
 
         @pl.when(g <= nz)
         def _():
-            each(g, use)
             if pair:
-                each(g, lambda zs, xs: add_up(zs * nx + xs))
+                multiply(g)
+            else:
+                each(g, use)
 
         if pair:
             @pl.when(g > 1)

time: 42.9 us -> 42.7 us (level)
  no operation moved by 1% of the time
where the time goes in v4:
time: 42.7 us; the launch traced here: 42.3 us
  Pallas kernels  40.4 us (95%)
  local copies, waits for them, and re-layouts  1.87 us (4%)
    pallas_call x1, Pallas kernels, shards(): pl.pallas_call(functools.partial(kernel, n, m), out_shape=jax.ShapeDtypeS...  40.4 us
    unnamed x1, local copies, waits for them, and re-layouts  1.87 us

profile of v4, /device:TPU:0, one launch (start us, length us, event | category | flops | bytes accessed | tf_op | source)
XLA Modules:
  0.0 42.3 jit_solution(14516254111927675252)
XLA Ops:
  0.0 40.4 %shard_map.82 = bf16[4,256,256]{2,1,0:T(8,128)(2,1)} custom-call(s32[16]{0:T(128)} %bitcast.9, s32[8]{0:T(128)} %place.1, s32[8]{0:T(128)} %left_sizes.1, s32[8]{0:T(128)} %right_sizes.1, bf16[2,16,16]{2,1,0:T(8,128)(2,1)} %ops.1, bf16[16,256,256]{2,1,0:T(8,128)(2,1)} %bitcast.5, bf16[2,256,256]{2,1,0:T(8,128)(2,1)} %bitcast.7, bf16[2,256,256]{2,1,0:T(8,128)(2,1)} %bitcast.8), custom_call_target="tpu_custom_call" | custom-call | tf_op jit(solution)/shard_map/pallas_call | solution.py:417
  40.4 1.9 %copy.10 = bf16[1,4,256,256]{3,2,1,0:T(8,128)(2,1)} copy(bf16[1,4,256,256]{3,2,1,0:T(8,128)(2,1)} %bitcast.6) | data formatting | bytes 1048576
